TPU v7x, 32 devices: a whole 2x2x4 slice. The times are simulated.
32 devices in a mesh: shell: 8 (over z, core), patch: 4 (over y, x).
Axes of the slice: x: 2, y: 2, z: 4, core: 2. Of those that a mesh axis runs over, the one named last changes fastest.
Arguments:
- field_j: float32 [2, 256, 128, 128], P(None, 'shell', 'patch'), may hold values from -1 to 1
Outputs:
- beta_field: float32 [256, 128, 128], P('shell', 'patch')
- u_field: float32 [2, 256, 128, 128], P(None, 'shell', 'patch')
- w_field: float32 [256, 128, 128], P('shell', 'patch')
- h_field: float32 [2, 256, 128, 128], P(None, 'shell', 'patch')
All inputs are finite; a program needn't handle non-finite values.
Results may differ from a plain program's by a relative error of at most 0.00002.
Values sent between devices are 32-bit elements; how exact they have to be, the bound alone decides.
A program may use at most 64 MiB of HBM per device.

v0:
```python
import math
import jax
import jax.numpy as jnp
from jax import lax
from jax.sharding import PartitionSpec as P


def shifted(block, axis, distance):
    devices = range(lax.axis_size(axis))
    route = [(i - distance, i) for i in devices if i - distance in devices]
    return lax.ppermute(block, axis, route)


def with_halo(shard, sides, width):
    for axis, dim in sides:
        size, length = (lax.axis_size(axis), shard.shape[dim])
        up = [(i, (i + 1) % size) for i in range(size)]
        down = [(j, i) for i, j in up]
        last = lax.slice_in_dim(shard, length - width, length, axis=dim)
        first = lax.slice_in_dim(shard, 0, width, axis=dim)
        before = lax.ppermute(last, axis, up)
        after = lax.ppermute(first, axis, down)
        shard = jnp.concatenate([before, shard, after], axis=dim)
    return shard


def theta_diff(values):
    zero_col = jnp.zeros(values.shape[:-1] + (1,), values.dtype)
    forward = jnp.concatenate([values[..., 1:], zero_col], axis=-1)
    backward = jnp.concatenate([zero_col, values[..., :-1]], axis=-1)
    return 0.5 * (forward - backward)


def crop(values, margin):
    return values[..., margin : values.shape[-2] - margin, :]


def phi_diff(values):
    return 0.5 * (values[..., 2:, :] - values[..., :-2, :])


def spin_diff(real_part, imag_part, orient):
    return (
        theta_diff(crop(real_part, 1)) - orient * phi_diff(imag_part),
        theta_diff(crop(imag_part, 1)) + orient * phi_diff(real_part),
    )


def earlier_total(gathered):
    shells = gathered.shape[0]
    keep_rows = jnp.arange(shells) < lax.axis_index("shell")
    keep_rows = keep_rows.reshape((shells,) + (1,) * (gathered.ndim - 1))
    return jnp.sum(jnp.where(keep_rows, gathered, 0.0), axis=0)


def cumulate(source, below_sum, radial_step):
    return radial_step * (jnp.cumsum(source, axis=-3) + jnp.expand_dims(below_sum, -3))


def beta_integral(source, radial_step):
    shell_sum = jnp.sum(source, axis=-3)
    gathered = lax.all_gather(shell_sum[None], "shell", axis=0, tiled=True)
    below_sum = earlier_total(gathered)
    return cumulate(source, below_sum, radial_step)


def u_integral(source, radial_step):
    shell_sum = jnp.sum(source, axis=-3)
    gathered = lax.all_gather(shell_sum[None], "shell", axis=0, tiled=True)
    below_sum = earlier_total(gathered)
    return cumulate(source, below_sum, radial_step)


def wh_integral(source_w, source_h, radial_step):
    sum_w = jnp.sum(source_w, axis=-3)
    sum_h = jnp.sum(source_h, axis=-3)
    gathered_w, gathered_h = (
        lax.all_gather(sum_w[None], "shell", axis=0, tiled=True),
        lax.all_gather(sum_h[None], "shell", axis=0, tiled=True),
    )
    below_w = earlier_total(gathered_w)
    below_h = earlier_total(gathered_h)
    return (cumulate(source_w, below_w, radial_step), cumulate(source_h, below_h, radial_step))


def source_beta(radial, eth_a, eth_b):
    return 0.25 * (
        0.5 * (radial[0] * radial[0] + radial[1] * radial[1]) - (eth_a * eth_a + eth_b * eth_b)
    )


def source_u(beta_field, beta_re, beta_im, field_j):
    growth = jnp.exp(2.0 * beta_field)
    field_a = field_j[0]
    field_b = field_j[1]
    source_ua = growth * (beta_re - (field_a * beta_re + field_b * beta_im))
    source_ub = growth * (beta_im - (field_b * beta_re - field_a * beta_im))
    return jnp.stack([source_ua, source_ub])


def local(field_j):
    radii_dev = field_j.shape[1]
    shells = lax.axis_size("shell")
    radial_step = 1.0 / math.sqrt(radii_dev * shells)
    arrived = shifted(field_j[:, :1], "shell", -1)
    outermost = lax.axis_index("shell") == shells - 1
    beyond = jnp.where(outermost, field_j[:, -1:], arrived)
    extended = jnp.concatenate([field_j, beyond], axis=1)
    field_rim = with_halo(field_j, (("patch", 2),), 1)
    radial = extended[:, 1:] - extended[:, :-1]
    eth_a, eth_b = spin_diff(field_rim[0], field_rim[1], 1.0)
    barj_a, barj_b = spin_diff(field_rim[0], field_rim[1], -1.0)
    beta_field = beta_integral(source_beta(radial, eth_a, eth_b), radial_step)
    beta_rim = with_halo(beta_field[None], (("patch", 2),), 1)[0]
    beta_re = theta_diff(beta_field)
    beta_im = phi_diff(beta_rim)
    u_field = u_integral(source_u(beta_field, beta_re, beta_im, field_j), radial_step)
    u_rim = with_halo(u_field, (("patch", 2),), 1)
    ethu_a, ethu_b = spin_diff(u_rim[0], u_rim[1], 1.0)
    baru_a, baru_b = spin_diff(u_rim[0], u_rim[1], -1.0)
    growth = jnp.exp(2.0 * beta_field)
    field_a = field_j[0]
    field_b = field_j[1]
    u_a = u_field[0]
    u_b = u_field[1]
    source_w = growth * baru_a + (field_b * u_a - field_a * u_b)
    source_ha = ethu_a + u_a * barj_a - u_b * barj_b + beta_field * field_a
    source_hb = ethu_b + u_a * barj_b + u_b * barj_a + beta_field * field_b
    w_field, h_field = wh_integral(source_w, jnp.stack([source_ha, source_hb]), radial_step)
    return (beta_field, u_field, w_field, h_field)


def solution(mesh):
    return jax.shard_map(
        local,
        mesh=mesh,
        in_specs=(P(None, "shell", "patch", None),),
        out_specs=(
            P("shell", "patch", None),
            P(None, "shell", "patch", None),
            P("shell", "patch", None),
            P(None, "shell", "patch", None),
        ),
        check_vma=False,
    )
```

profile of v0, /device:TPU:0, one launch (start us, length us, event | category | flops | bytes accessed | tf_op | source)
XLA Modules:
  0.0 89.5 jit_solution(15195173211261060184)
XLA Ops:
  0.6 0.9 slice.153
  1.5 1.3 %collective-permute-start = (f32[2,1,32,128]{3,2,1,0:T(8,128)S(1)}, f32[2,1,32,128]{3,2,1,0:T(8,128)S(1)}, u32[]{:S(2)}, u32[]{:S(2)}) collective-permute-start(f32[2,1,32,128]{3,2,1,0:T(8,128)S(1)} %slice.153), channel_id=1, source_target_pairs={{4,0},{8,4},{12,8},{16,12},{20,16},{24,20},{28,24},{5,1},{9,5},{13... | collective-permute-start | bytes 98312 | tf_op jit(solution)/shard_map/ppermute | solution.py:11
  2.8 1.1 %fusion.38 = (f32[2,32,1,128]{3,2,1,0:T(1,128)S(1)}, f32[2,32,1,128]{3,2,1,0:T(1,128)S(1)}) fusion(f32[2,32,32,128]{3,2,1,0:T(8,128)} %param.1), kind=kLoop, calls=%fused_computation.81 | loop fusion | bytes 131072 | tf_op jit(solution)/shard_map/slice | solution.py:19
  3.9 3.0 %collective-permute-start.1 = (f32[2,32,1,128]{3,2,1,0:T(1,128)S(1)}, f32[2,32,1,128]{3,2,1,0:T(1,128)S(1)}, u32[]{:S(2)}, u32[]{:S(2)}) collective-permute-start(f32[2,32,1,128]{3,2,1,0:T(1,128)S(1)} %get-tuple-element.16), channel_id=1, source_target_pairs={{0,1},{1,2},{2,3},{3,0},{4,5},{5,6},{6,7},{7,4},{8,9},{9,10},{10,1... | collective-permute-start | bytes 98312 | tf_op jit(solution)/shard_map/ppermute | solution.py:21
  6.9 1.0 %collective-permute-start.2 = (f32[2,32,1,128]{3,2,1,0:T(1,128)S(1)}, f32[2,32,1,128]{3,2,1,0:T(1,128)S(1)}, u32[]{:S(2)}, u32[]{:S(2)}) collective-permute-start(f32[2,32,1,128]{3,2,1,0:T(1,128)S(1)} %get-tuple-element.17), channel_id=1, source_target_pairs={{1,0},{2,1},{3,2},{0,3},{5,4},{6,5},{7,6},{4,7},{9,8},{10,9},{11,1... | collective-permute-start | bytes 98312 | tf_op jit(solution)/shard_map/ppermute | solution.py:22
  7.9 0.8 slice_select_fusion
  8.7 1.9 %fusion = f32[2,32,32,128]{3,2,1,0:T(8,128)S(1)} fusion(f32[2,32,32,128]{3,2,1,0:T(8,128)} %param.1, f32[2,1,32,128]{3,2,1,0:T(8,128)S(1)} %slice_select_fusion), kind=kLoop, calls=%fused_computation.3 | loop fusion | flops 524288 | bytes 2129920 | tf_op jit(solution)/shard_map/sub | solution.py:110
  12.5 14.7 %all-gather = f32[256,128]{1,0:T(8,128)S(1)} all-gather(f32[32,128]{1,0:T(8,128)S(1)} %get-tuple-element.6), channel_id=2, replica_groups=mesh['shell'=8,'patch'=4] {'shell'}, dimensions={0}, use_global_device_ids=true | all-gather | bytes 147456 | tf_op jit(solution)/shard_map/all_gather | solution.py:62
  27.2 1.9 %fusion.45 = f32[32,32,128]{2,1,0:T(8,128)S(1)} fusion(f32[32,32,128]{2,1,0:T(8,128)S(1)} %get-tuple-element.7), kind=kOutput, calls=%fused_computation.88 | output fusion | flops 4063232 | bytes 1048576 | tf_op jit(solution)/shard_map/jit(cumsum)/reduce_window_sum | solution.py:57
  29.4 2.3 %collective-permute-start.3 = (f32[1,32,1,128]{3,2,1,0:T(1,128)S(1)}, f32[1,32,1,128]{3,2,1,0:T(1,128)S(1)}, u32[]{:S(2)}, u32[]{:S(2)}) collective-permute-start(f32[1,32,1,128]{3,2,1,0:T(1,128)S(1)} %get-tuple-element.26), channel_id=1, source_target_pairs={{0,1},{1,2},{2,3},{3,0},{4,5},{5,6},{6,7},{7,4},{8,9},{9,10},{10,1... | collective-permute-start | bytes 49160 | tf_op jit(solution)/shard_map/ppermute | solution.py:21
  31.6 0.7 collective-permute-start.4
  32.6 1.5 %collective-permute-done.3 = f32[1,32,1,128]{3,2,1,0:T(1,128)S(1)} collective-permute-done((f32[1,32,1,128]{3,2,1,0:T(1,128)S(1)}, f32[1,32,1,128]{3,2,1,0:T(1,128)S(1)}, u32[]{:S(2)}, u32[]{:S(2)}) %collective-permute-start.3) | collective-permute-done | bytes 16416 | tf_op jit(solution)/shard_map/ppermute | solution.py:21
  34.1 1.3 %collective-permute-done.4 = f32[1,32,1,128]{3,2,1,0:T(1,128)S(1)} collective-permute-done((f32[1,32,1,128]{3,2,1,0:T(1,128)S(1)}, f32[1,32,1,128]{3,2,1,0:T(1,128)S(1)}, u32[]{:S(2)}, u32[]{:S(2)}) %collective-permute-start.4) | collective-permute-done | bytes 16416 | tf_op jit(solution)/shard_map/ppermute | solution.py:22
  36.0 14.3 %all-gather.1 = f32[16,32,128]{2,1,0:T(8,128)S(1)} all-gather(f32[2,32,128]{2,1,0:T(8,128)S(1)} %fusion.3), channel_id=3, replica_groups=mesh['shell'=8,'patch'=4] {'shell'}, dimensions={0}, use_global_device_ids=true | all-gather | bytes 294912 | tf_op jit(solution)/shard_map/all_gather | solution.py:69
  50.6 1.7 %collective-permute-start.5 = (f32[2,32,1,128]{3,2,1,0:T(1,128)S(1)}, f32[2,32,1,128]{3,2,1,0:T(1,128)S(1)}, u32[]{:S(2)}, u32[]{:S(2)}) collective-permute-start(f32[2,32,1,128]{3,2,1,0:T(1,128)S(1)} %get-tuple-element.14), channel_id=1, source_target_pairs={{0,1},{1,2},{2,3},{3,0},{4,5},{5,6},{6,7},{7,4},{8,9},{9,10},{10,1... | collective-permute-start | bytes 98312 | tf_op jit(solution)/shard_map/ppermute | solution.py:21
  52.4 1.2 %collective-permute-start.6 = (f32[2,32,1,128]{3,2,1,0:T(1,128)S(1)}, f32[2,32,1,128]{3,2,1,0:T(1,128)S(1)}, u32[]{:S(2)}, u32[]{:S(2)}) collective-permute-start(f32[2,32,1,128]{3,2,1,0:T(1,128)S(1)} %get-tuple-element.15), channel_id=1, source_target_pairs={{1,0},{2,1},{3,2},{0,3},{5,4},{6,5},{7,6},{4,7},{9,8},{10,9},{11,1... | collective-permute-start | bytes 98312 | tf_op jit(solution)/shard_map/ppermute | solution.py:22
  53.6 2.1 %collective-permute-done.5 = f32[2,32,1,128]{3,2,1,0:T(1,128)S(1)} collective-permute-done((f32[2,32,1,128]{3,2,1,0:T(1,128)S(1)}, f32[2,32,1,128]{3,2,1,0:T(1,128)S(1)}, u32[]{:S(2)}, u32[]{:S(2)}) %collective-permute-start.5) | collective-permute-done | bytes 32800 | tf_op jit(solution)/shard_map/ppermute | solution.py:21
  55.7 0.6 collective-permute-done.6
  56.8 0.8 fusion.30
  58.3 14.1 %all-gather.2 = f32[256,128]{1,0:T(8,128)S(1)} all-gather(f32[32,128]{1,0:T(8,128)S(1)} %get-tuple-element.4), channel_id=4, replica_groups=mesh['shell'=8,'patch'=4] {'shell'}, dimensions={0}, use_global_device_ids=true | all-gather | bytes 147456 | tf_op jit(solution)/shard_map/all_gather | solution.py:78
  72.4 0.8 fusion.11
  73.3 14.2 %all-gather.3 = f32[16,32,128]{2,1,0:T(8,128)S(1)} all-gather(f32[2,32,128]{2,1,0:T(8,128)S(1)} %fusion.1), channel_id=5, replica_groups=mesh['shell'=8,'patch'=4] {'shell'}, dimensions={0}, use_global_device_ids=true | all-gather | bytes 294912 | tf_op jit(solution)/shard_map/all_gather | solution.py:79
  87.6 1.1 %add_multiply_fusion = f32[2,32,32,128]{3,2,1,0:T(8,128)} fusion(f32[1,32,32,128]{3,2,1,0:T(8,128)S(1)} %fusion.11, f32[1,32,32,128]{3,2,1,0:T(8,128)S(1)} %fusion.30, f32[2,32,128]{2,1,0:T(8,128)S(1)} %select_reduce_fusion), kind=kOutput, calls=%fused_computation.6 | output fusion | flops 8912896 | bytes 2129920 | tf_op jit(solution)/shard_map/jit(cumsum)/reduce_window_sum | solution.py:57
  88.7 0.9 fusion.5
  (33 shorter events, 4.6 us)
Async XLA Ops:
  0.6 10.5 %copy-start = (f32[2,32,32,128]{3,2,1,0:T(8,128)S(1)}, f32[2,32,32,128]{3,2,1,0:T(8,128)}, u32[]{:S(2)}) copy-start(f32[2,32,32,128]{3,2,1,0:T(8,128)} %param.1) | copy-start | bytes 3145732
  1.5 6.4 %collective-permute-start = (f32[2,1,32,128]{3,2,1,0:T(8,128)S(1)}, f32[2,1,32,128]{3,2,1,0:T(8,128)S(1)}, u32[]{:S(2)}, u32[]{:S(2)}) collective-permute-start(f32[2,1,32,128]{3,2,1,0:T(8,128)S(1)} %slice.153), channel_id=1, source_target_pairs={{4,0},{8,4},{12,8},{16,12},{20,16},{24,20},{28,24},{5,1},{9,5},{13... | collective-permute-start | bytes 98312 | tf_op jit(solution)/shard_map/ppermute | solution.py:11
  3.9 6.7 %collective-permute-start.1 = (f32[2,32,1,128]{3,2,1,0:T(1,128)S(1)}, f32[2,32,1,128]{3,2,1,0:T(1,128)S(1)}, u32[]{:S(2)}, u32[]{:S(2)}) collective-permute-start(f32[2,32,1,128]{3,2,1,0:T(1,128)S(1)} %get-tuple-element.16), channel_id=1, source_target_pairs={{0,1},{1,2},{2,3},{3,0},{4,5},{5,6},{6,7},{7,4},{8,9},{9,10},{10,1... | collective-permute-start | bytes 98312 | tf_op jit(solution)/shard_map/ppermute | solution.py:21
  6.9 4.3 %collective-permute-start.2 = (f32[2,32,1,128]{3,2,1,0:T(1,128)S(1)}, f32[2,32,1,128]{3,2,1,0:T(1,128)S(1)}, u32[]{:S(2)}, u32[]{:S(2)}) collective-permute-start(f32[2,32,1,128]{3,2,1,0:T(1,128)S(1)} %get-tuple-element.17), channel_id=1, source_target_pairs={{1,0},{2,1},{3,2},{0,3},{5,4},{6,5},{7,6},{4,7},{9,8},{10,9},{11,1... | collective-permute-start | bytes 98312 | tf_op jit(solution)/shard_map/ppermute | solution.py:22
  29.3 6.1 %copy-start.2 = (f32[32,32,128]{2,1,0:T(8,128)}, f32[32,32,128]{2,1,0:T(8,128)S(1)}, u32[]{:S(2)}) copy-start(f32[32,32,128]{2,1,0:T(8,128)S(1)} %add_multiply_fusion.2) | copy-start | bytes 1572868
  29.4 4.7 %collective-permute-start.3 = (f32[1,32,1,128]{3,2,1,0:T(1,128)S(1)}, f32[1,32,1,128]{3,2,1,0:T(1,128)S(1)}, u32[]{:S(2)}, u32[]{:S(2)}) collective-permute-start(f32[1,32,1,128]{3,2,1,0:T(1,128)S(1)} %get-tuple-element.26), channel_id=1, source_target_pairs={{0,1},{1,2},{2,3},{3,0},{4,5},{5,6},{6,7},{7,4},{8,9},{9,10},{10,1... | collective-permute-start | bytes 49160 | tf_op jit(solution)/shard_map/ppermute | solution.py:21
  31.6 3.7 %collective-permute-start.4 = (f32[1,32,1,128]{3,2,1,0:T(1,128)S(1)}, f32[1,32,1,128]{3,2,1,0:T(1,128)S(1)}, u32[]{:S(2)}, u32[]{:S(2)}) collective-permute-start(f32[1,32,1,128]{3,2,1,0:T(1,128)S(1)} %get-tuple-element.27), channel_id=1, source_target_pairs={{1,0},{2,1},{3,2},{0,3},{5,4},{6,5},{7,6},{4,7},{9,8},{10,9},{11,1... | collective-permute-start | bytes 49160 | tf_op jit(solution)/shard_map/ppermute | solution.py:22
  50.6 21.8 %copy-start.1 = (f32[2,32,32,128]{3,2,1,0:T(8,128)}, f32[2,32,32,128]{3,2,1,0:T(8,128)S(1)}, u32[]{:S(2)}) copy-start(f32[2,32,32,128]{3,2,1,0:T(8,128)S(1)} %add_multiply_fusion.1) | copy-start | bytes 3145732
  50.6 5.0 %collective-permute-start.5 = (f32[2,32,1,128]{3,2,1,0:T(1,128)S(1)}, f32[2,32,1,128]{3,2,1,0:T(1,128)S(1)}, u32[]{:S(2)}, u32[]{:S(2)}) collective-permute-start(f32[2,32,1,128]{3,2,1,0:T(1,128)S(1)} %get-tuple-element.14), channel_id=1, source_target_pairs={{0,1},{1,2},{2,3},{3,0},{4,5},{5,6},{6,7},{7,4},{8,9},{9,10},{10,1... | collective-permute-start | bytes 98312 | tf_op jit(solution)/shard_map/ppermute | solution.py:21
  52.4 3.9 %collective-permute-start.6 = (f32[2,32,1,128]{3,2,1,0:T(1,128)S(1)}, f32[2,32,1,128]{3,2,1,0:T(1,128)S(1)}, u32[]{:S(2)}, u32[]{:S(2)}) collective-permute-start(f32[2,32,1,128]{3,2,1,0:T(1,128)S(1)} %get-tuple-element.15), channel_id=1, source_target_pairs={{1,0},{2,1},{3,2},{0,3},{5,4},{6,5},{7,6},{4,7},{9,8},{10,9},{11,1... | collective-permute-start | bytes 98312 | tf_op jit(solution)/shard_map/ppermute | solution.py:22
where the time goes:
time: 89.8 us; the launch traced here: 89.5 us
  blocking collectives  57.3 us (64%)
  starting transfers between devices  11.3 us (13%)
  other arithmetic  10.8 us (12%)
  waiting for transfers between devices  6.09 us (7%)
  local copies, waits for them, and re-layouts  3.27 us (4%)
    all_gather x1, blocking collectives, beta_integral(): gathered = lax.all_gather(shell_sum[None], 'shell', axis=0, tiled=True)  14.7 us
    all_gather x1, blocking collectives, u_integral(): gathered = lax.all_gather(shell_sum[None], 'shell', axis=0, tiled=True)  14.3 us
    all_gather x1, blocking collectives, wh_integral(): lax.all_gather(sum_h[None], 'shell', axis=0, tiled=True)  14.2 us
    all_gather x1, blocking collectives, wh_integral(): lax.all_gather(sum_w[None], 'shell', axis=0, tiled=True)  14.1 us
    ppermute x3, starting transfers between devices, with_halo(): before = lax.ppermute(last, axis, up)  7 us
    another operation x4, other arithmetic, cumulate(): jnp.cumsum(source, axis=-3) + jnp.expand_dims(below_sum, -3)  4.01 us
    ppermute x3, waiting for transfers between devices, with_halo(): before = lax.ppermute(last, axis, up)  3.56 us
    ppermute x3, starting transfers between devices, with_halo(): after = lax.ppermute(first, axis, down)  2.99 us
  transfers between devices with their start and end apart: 7, of which 5 were waited for; matrix products, arithmetic and copies ran while one was open for 4% of the time, Pallas kernels for 0%

commit v1 on v0

--- a/solution.py
+++ b/solution.py
@@ -3,6 +3,16 @@
 import jax.numpy as jnp
 from jax import lax
 from jax.sharding import PartitionSpec as P
+
+
+def ring_gather(x, axis, dim):
+    ways, here, lap = (lax.axis_size(axis), lax.axis_index(axis), x.shape[dim])
+    dims = [n * ways if d == dim else n for d, n in enumerate(x.shape)]
+    full = lax.dynamic_update_slice_in_dim(jnp.zeros(dims, x.dtype), x, here * lap, axis=dim)
+    for far in range(1, ways):
+        x = lax.ppermute(x, axis, [(d, (d + 1) % ways) for d in range(ways)])
+        full = lax.dynamic_update_slice_in_dim(full, x, (here - far) % ways * lap, axis=dim)
+    return full
 
 
 def shifted(block, axis, distance):
@@ -76,7 +86,7 @@
     sum_h = jnp.sum(source_h, axis=-3)
     gathered_w, gathered_h = (
         lax.all_gather(sum_w[None], "shell", axis=0, tiled=True),
-        lax.all_gather(sum_h[None], "shell", axis=0, tiled=True),
+        ring_gather(sum_h[None], "shell", 0),
     )
     below_w = earlier_total(gathered_w)
     below_h = earlier_total(gathered_h)

time: 89.8 us -> 113 us (1.26)
  waiting for transfers between devices: 6.09 us -> 40.8 us
  blocking collectives: 57.3 us -> 43 us
  local copies, waits for them, and re-layouts: 3.27 us -> 5.33 us
    ppermute x0 -> x7, waiting for transfers between devices: none -> 34.6 us  [ring_gather(): x = lax.ppermute(x, axis, [(d, (d + 1) % ways) for d in range(ways)])]
    all_gather x1 -> x0, blocking collectives: 14.2 us -> none  [wh_integral(): lax.all_gather(sum_h[None], 'shell', axis=0, tiled=True)]
    unnamed x6 -> x30, local copies, waits for them, and re-layouts: 0.02 us -> 2.02 us
  transfers between devices with their start and end apart: 7 -> 14, of which waited for: 5 -> 12; matrix products, arithmetic and copies ran while one was open for 4% -> 4% of each run, Pallas kernels for 0% -> 0%
where the time goes in v1:
time: 113 us
  blocking collectives  43 us (38%)
  waiting for transfers between devices  40.8 us (36%)
  starting transfers between devices  11.7 us (10%)
  other arithmetic  10.7 us (9%)
  local copies, waits for them, and re-layouts  5.33 us (5%)
    ppermute x7, waiting for transfers between devices, ring_gather(): x = lax.ppermute(x, axis, [(d, (d + 1) % ways) for d in range(ways)])  34.6 us
    all_gather x1, blocking collectives, beta_integral(): gathered = lax.all_gather(shell_sum[None], 'shell', axis=0, tiled=True)  14.6 us
    all_gather x1, blocking collectives, u_integral(): gathered = lax.all_gather(shell_sum[None], 'shell', axis=0, tiled=True)  14.3 us
    all_gather x1, blocking collectives, wh_integral(): lax.all_gather(sum_w[None], 'shell', axis=0, tiled=True)  14.1 us
    ppermute x3, starting transfers between devices, with_halo(): before = lax.ppermute(last, axis, up)  7 us
    another operation x4, other arithmetic, cumulate(): jnp.cumsum(source, axis=-3) + jnp.expand_dims(below_sum, -3)  4.01 us
    ppermute x3, waiting for transfers between devices, with_halo(): before = lax.ppermute(last, axis, up)  3.49 us
    ppermute x3, starting transfers between devices, with_halo(): after = lax.ppermute(first, axis, down)  2.99 us
  transfers between devices with their start and end apart: 14, of which 12 were waited for; matrix products, arithmetic and copies ran while one was open for 4% of the time, Pallas kernels for 0%

profile of v1, /device:TPU:0, one launch (start us, length us, event | category | flops | bytes accessed | tf_op | source)
XLA Modules:
  0.0 112.5 jit_solution(2005084782510075903)
XLA Ops:
  1.5 1.3 %collective-permute-start = (f32[2,1,32,128]{3,2,1,0:T(8,128)S(1)}, f32[2,1,32,128]{3,2,1,0:T(8,128)S(1)}, u32[]{:S(2)}, u32[]{:S(2)}) collective-permute-start(f32[2,1,32,128]{3,2,1,0:T(8,128)S(1)} %slice.153), channel_id=1, source_target_pairs={{4,0},{8,4},{12,8},{16,12},{20,16},{24,20},{28,24},{5,1},{9,5},{13... | collective-permute-start | bytes 98312 | tf_op jit(solution)/shard_map/ppermute | solution.py:21
  2.8 1.1 fusion.38
  3.9 3.0 %collective-permute-start.1 = (f32[2,32,1,128]{3,2,1,0:T(1,128)S(1)}, f32[2,32,1,128]{3,2,1,0:T(1,128)S(1)}, u32[]{:S(2)}, u32[]{:S(2)}) collective-permute-start(f32[2,32,1,128]{3,2,1,0:T(1,128)S(1)} %get-tuple-element.16), channel_id=1, source_target_pairs={{0,1},{1,2},{2,3},{3,0},{4,5},{5,6},{6,7},{7,4},{8,9},{9,10},{10,1... | collective-permute-start | bytes 98312 | tf_op jit(solution)/shard_map/ppermute | solution.py:31
  6.9 1.0 collective-permute-start.2
  8.7 1.8 %fusion = f32[2,32,32,128]{3,2,1,0:T(8,128)S(1)} fusion(f32[2,32,32,128]{3,2,1,0:T(8,128)} %param.1, f32[2,1,32,128]{3,2,1,0:T(8,128)S(1)} %slice_select_fusion), kind=kLoop, calls=%fused_computation.3 | loop fusion | flops 524288 | bytes 2129920 | tf_op jit(solution)/shard_map/sub | solution.py:120
  13.2 14.6 %all-gather = f32[256,128]{1,0:T(8,128)S(1)} all-gather(f32[32,128]{1,0:T(8,128)S(1)} %get-tuple-element.6), channel_id=2, replica_groups=mesh['shell'=8,'patch'=4] {'shell'}, dimensions={0}, use_global_device_ids=true | all-gather | bytes 147456 | tf_op jit(solution)/shard_map/all_gather | solution.py:72
  27.8 1.9 %fusion.45 = f32[32,32,128]{2,1,0:T(8,128)S(1)} fusion(f32[32,32,128]{2,1,0:T(8,128)S(1)} %get-tuple-element.7), kind=kOutput, calls=%fused_computation.96 | output fusion | flops 4063232 | bytes 1048576 | tf_op jit(solution)/shard_map/jit(cumsum)/reduce_window_sum | solution.py:67
  30.0 2.3 %collective-permute-start.3 = (f32[1,32,1,128]{3,2,1,0:T(1,128)S(1)}, f32[1,32,1,128]{3,2,1,0:T(1,128)S(1)}, u32[]{:S(2)}, u32[]{:S(2)}) collective-permute-start(f32[1,32,1,128]{3,2,1,0:T(1,128)S(1)} %get-tuple-element.26), channel_id=1, source_target_pairs={{0,1},{1,2},{2,3},{3,0},{4,5},{5,6},{6,7},{7,4},{8,9},{9,10},{10,1... | collective-permute-start | bytes 49160 | tf_op jit(solution)/shard_map/ppermute | solution.py:31
  33.2 1.5 %collective-permute-done.3 = f32[1,32,1,128]{3,2,1,0:T(1,128)S(1)} collective-permute-done((f32[1,32,1,128]{3,2,1,0:T(1,128)S(1)}, f32[1,32,1,128]{3,2,1,0:T(1,128)S(1)}, u32[]{:S(2)}, u32[]{:S(2)}) %collective-permute-start.3) | collective-permute-done | bytes 16416 | tf_op jit(solution)/shard_map/ppermute | solution.py:31
  34.7 1.4 %collective-permute-done.4 = f32[1,32,1,128]{3,2,1,0:T(1,128)S(1)} collective-permute-done((f32[1,32,1,128]{3,2,1,0:T(1,128)S(1)}, f32[1,32,1,128]{3,2,1,0:T(1,128)S(1)}, u32[]{:S(2)}, u32[]{:S(2)}) %collective-permute-start.4) | collective-permute-done | bytes 16416 | tf_op jit(solution)/shard_map/ppermute | solution.py:32
  36.8 14.3 %all-gather.1 = f32[16,32,128]{2,1,0:T(8,128)S(1)} all-gather(f32[2,32,128]{2,1,0:T(8,128)S(1)} %fusion.3), channel_id=3, replica_groups=mesh['shell'=8,'patch'=4] {'shell'}, dimensions={0}, use_global_device_ids=true | all-gather | bytes 294912 | tf_op jit(solution)/shard_map/all_gather | solution.py:79
  51.4 1.7 %collective-permute-start.5 = (f32[2,32,1,128]{3,2,1,0:T(1,128)S(1)}, f32[2,32,1,128]{3,2,1,0:T(1,128)S(1)}, u32[]{:S(2)}, u32[]{:S(2)}) collective-permute-start(f32[2,32,1,128]{3,2,1,0:T(1,128)S(1)} %get-tuple-element.14), channel_id=1, source_target_pairs={{0,1},{1,2},{2,3},{3,0},{4,5},{5,6},{6,7},{7,4},{8,9},{9,10},{10,1... | collective-permute-start | bytes 98312 | tf_op jit(solution)/shard_map/ppermute | solution.py:31
  53.0 1.3 %collective-permute-start.6 = (f32[2,32,1,128]{3,2,1,0:T(1,128)S(1)}, f32[2,32,1,128]{3,2,1,0:T(1,128)S(1)}, u32[]{:S(2)}, u32[]{:S(2)}) collective-permute-start(f32[2,32,1,128]{3,2,1,0:T(1,128)S(1)} %get-tuple-element.15), channel_id=1, source_target_pairs={{1,0},{2,1},{3,2},{0,3},{5,4},{6,5},{7,6},{4,7},{9,8},{10,9},{11,1... | collective-permute-start | bytes 98312 | tf_op jit(solution)/shard_map/ppermute | solution.py:32
  54.3 2.0 %collective-permute-done.5 = f32[2,32,1,128]{3,2,1,0:T(1,128)S(1)} collective-permute-done((f32[2,32,1,128]{3,2,1,0:T(1,128)S(1)}, f32[2,32,1,128]{3,2,1,0:T(1,128)S(1)}, u32[]{:S(2)}, u32[]{:S(2)}) %collective-permute-start.5) | collective-permute-done | bytes 32800 | tf_op jit(solution)/shard_map/ppermute | solution.py:31
  60.3 14.1 %all-gather.2 = f32[256,128]{1,0:T(8,128)S(1)} all-gather(f32[32,128]{1,0:T(8,128)S(1)} %get-tuple-element.4), channel_id=4, replica_groups=mesh['shell'=8,'patch'=4] {'shell'}, dimensions={0}, use_global_device_ids=true | all-gather | bytes 147456 | tf_op jit(solution)/shard_map/all_gather | solution.py:88
  75.7 0.9 fusion.5
  76.6 3.9 %collective-permute-done.7 = f32[1,2,32,128]{3,2,1,0:T(8,128)S(1)} collective-permute-done((f32[1,2,32,128]{3,2,1,0:T(8,128)S(1)}, f32[1,2,32,128]{3,2,1,0:T(8,128)S(1)}, u32[]{:S(2)}, u32[]{:S(2)}) %collective-permute-start.7) | collective-permute-done | bytes 32800 | tf_op jit(solution)/shard_map/ppermute | solution.py:13
  80.5 5.1 %collective-permute-done.8 = f32[1,2,32,128]{3,2,1,0:T(8,128)S(1)} collective-permute-done((f32[1,2,32,128]{3,2,1,0:T(8,128)S(1)}, f32[1,2,32,128]{3,2,1,0:T(8,128)S(1)}, u32[]{:S(2)}, u32[]{:S(2)}) %collective-permute-start.8) | collective-permute-done | bytes 32800 | tf_op jit(solution)/shard_map/ppermute | solution.py:13
  85.7 5.1 %collective-permute-done.9 = f32[1,2,32,128]{3,2,1,0:T(8,128)S(1)} collective-permute-done((f32[1,2,32,128]{3,2,1,0:T(8,128)S(1)}, f32[1,2,32,128]{3,2,1,0:T(8,128)S(1)}, u32[]{:S(2)}, u32[]{:S(2)}) %collective-permute-start.9) | collective-permute-done | bytes 32800 | tf_op jit(solution)/shard_map/ppermute | solution.py:13
  90.8 5.1 %collective-permute-done.10 = f32[1,2,32,128]{3,2,1,0:T(8,128)S(1)} collective-permute-done((f32[1,2,32,128]{3,2,1,0:T(8,128)S(1)}, f32[1,2,32,128]{3,2,1,0:T(8,128)S(1)}, u32[]{:S(2)}, u32[]{:S(2)}) %collective-permute-start.10) | collective-permute-done | bytes 32800 | tf_op jit(solution)/shard_map/ppermute | solution.py:13
  95.9 5.1 %collective-permute-done.11 = f32[1,2,32,128]{3,2,1,0:T(8,128)S(1)} collective-permute-done((f32[1,2,32,128]{3,2,1,0:T(8,128)S(1)}, f32[1,2,32,128]{3,2,1,0:T(8,128)S(1)}, u32[]{:S(2)}, u32[]{:S(2)}) %collective-permute-start.11) | collective-permute-done | bytes 32800 | tf_op jit(solution)/shard_map/ppermute | solution.py:13
  101.1 5.1 %collective-permute-done.12 = f32[1,2,32,128]{3,2,1,0:T(8,128)S(1)} collective-permute-done((f32[1,2,32,128]{3,2,1,0:T(8,128)S(1)}, f32[1,2,32,128]{3,2,1,0:T(8,128)S(1)}, u32[]{:S(2)}, u32[]{:S(2)}) %collective-permute-start.12) | collective-permute-done | bytes 32800 | tf_op jit(solution)/shard_map/ppermute | solution.py:13
  106.2 5.1 %collective-permute-done.13 = f32[1,2,32,128]{3,2,1,0:T(8,128)S(1)} collective-permute-done((f32[1,2,32,128]{3,2,1,0:T(8,128)S(1)}, f32[1,2,32,128]{3,2,1,0:T(8,128)S(1)}, u32[]{:S(2)}, u32[]{:S(2)}) %collective-permute-start.13) | collective-permute-done | bytes 32800 | tf_op jit(solution)/shard_map/ppermute | solution.py:13
  111.4 1.1 add_multiply_fusion
  (79 shorter events, 11.7 us)
Async XLA Ops:
  0.6 10.5 %copy-start = (f32[2,32,32,128]{3,2,1,0:T(8,128)S(1)}, f32[2,32,32,128]{3,2,1,0:T(8,128)}, u32[]{:S(2)}) copy-start(f32[2,32,32,128]{3,2,1,0:T(8,128)} %param.1) | copy-start | bytes 3145732
  1.5 6.4 %collective-permute-start = (f32[2,1,32,128]{3,2,1,0:T(8,128)S(1)}, f32[2,1,32,128]{3,2,1,0:T(8,128)S(1)}, u32[]{:S(2)}, u32[]{:S(2)}) collective-permute-start(f32[2,1,32,128]{3,2,1,0:T(8,128)S(1)} %slice.153), channel_id=1, source_target_pairs={{4,0},{8,4},{12,8},{16,12},{20,16},{24,20},{28,24},{5,1},{9,5},{13... | collective-permute-start | bytes 98312 | tf_op jit(solution)/shard_map/ppermute | solution.py:21
  3.9 6.6 %collective-permute-start.1 = (f32[2,32,1,128]{3,2,1,0:T(1,128)S(1)}, f32[2,32,1,128]{3,2,1,0:T(1,128)S(1)}, u32[]{:S(2)}, u32[]{:S(2)}) collective-permute-start(f32[2,32,1,128]{3,2,1,0:T(1,128)S(1)} %get-tuple-element.16), channel_id=1, source_target_pairs={{0,1},{1,2},{2,3},{3,0},{4,5},{5,6},{6,7},{7,4},{8,9},{9,10},{10,1... | collective-permute-start | bytes 98312 | tf_op jit(solution)/shard_map/ppermute | solution.py:31
  6.9 4.3 %collective-permute-start.2 = (f32[2,32,1,128]{3,2,1,0:T(1,128)S(1)}, f32[2,32,1,128]{3,2,1,0:T(1,128)S(1)}, u32[]{:S(2)}, u32[]{:S(2)}) collective-permute-start(f32[2,32,1,128]{3,2,1,0:T(1,128)S(1)} %get-tuple-element.17), channel_id=1, source_target_pairs={{1,0},{2,1},{3,2},{0,3},{5,4},{6,5},{7,6},{4,7},{9,8},{10,9},{11,1... | collective-permute-start | bytes 98312 | tf_op jit(solution)/shard_map/ppermute | solution.py:32
  7.9 43.2 %copy-start.13 = (pred[8]{0:T(512)(128)(4,1)}, pred[8]{0:T(512)(128)(4,1)S(1)}, u32[]{:S(2)}) copy-start(pred[8]{0:T(512)(128)(4,1)S(1)} %iota_compare_fusion) | copy-start | bytes 28
  11.9 1.3 %copy-start.10 = (f32[32,32,127]{2,1,0:T(8,128)}, f32[32,32,127]{2,1,0:T(8,128)S(1)}, u32[]{:S(2)}) copy-start(f32[32,32,127]{2,1,0:T(8,128)S(1)} %get-tuple-element.31) | copy-start | bytes 1560580
  29.8 6.4 %copy-start.2 = (f32[32,32,128]{2,1,0:T(8,128)}, f32[32,32,128]{2,1,0:T(8,128)S(1)}, u32[]{:S(2)}) copy-start(f32[32,32,128]{2,1,0:T(8,128)S(1)} %fusion.45) | copy-start | bytes 1572868
  30.0 6.2 %copy-start.12 = (f32[32,32,128]{2,1,0:T(8,128)}, f32[32,32,128]{2,1,0:T(8,128)S(1)}, u32[]{:S(2)}) copy-start(f32[32,32,128]{2,1,0:T(8,128)S(1)} %add_multiply_fusion.2) | copy-start | bytes 1572868
  30.0 4.7 %collective-permute-start.3 = (f32[1,32,1,128]{3,2,1,0:T(1,128)S(1)}, f32[1,32,1,128]{3,2,1,0:T(1,128)S(1)}, u32[]{:S(2)}, u32[]{:S(2)}) collective-permute-start(f32[1,32,1,128]{3,2,1,0:T(1,128)S(1)} %get-tuple-element.26), channel_id=1, source_target_pairs={{0,1},{1,2},{2,3},{3,0},{4,5},{5,6},{6,7},{7,4},{8,9},{9,10},{10,1... | collective-permute-start | bytes 49160 | tf_op jit(solution)/shard_map/ppermute | solution.py:31
  32.4 3.7 %collective-permute-start.4 = (f32[1,32,1,128]{3,2,1,0:T(1,128)S(1)}, f32[1,32,1,128]{3,2,1,0:T(1,128)S(1)}, u32[]{:S(2)}, u32[]{:S(2)}) collective-permute-start(f32[1,32,1,128]{3,2,1,0:T(1,128)S(1)} %get-tuple-element.27), channel_id=1, source_target_pairs={{1,0},{2,1},{3,2},{0,3},{5,4},{6,5},{7,6},{4,7},{9,8},{10,9},{11,1... | collective-permute-start | bytes 49160 | tf_op jit(solution)/shard_map/ppermute | solution.py:32
  51.3 23.2 %copy-start.1 = (f32[2,32,32,128]{3,2,1,0:T(8,128)}, f32[2,32,32,128]{3,2,1,0:T(8,128)S(1)}, u32[]{:S(2)}) copy-start(f32[2,32,32,128]{3,2,1,0:T(8,128)S(1)} %add_multiply_fusion.1) | copy-start | bytes 3145732
  51.4 5.0 %collective-permute-start.5 = (f32[2,32,1,128]{3,2,1,0:T(1,128)S(1)}, f32[2,32,1,128]{3,2,1,0:T(1,128)S(1)}, u32[]{:S(2)}, u32[]{:S(2)}) collective-permute-start(f32[2,32,1,128]{3,2,1,0:T(1,128)S(1)} %get-tuple-element.14), channel_id=1, source_target_pairs={{0,1},{1,2},{2,3},{3,0},{4,5},{5,6},{6,7},{7,4},{8,9},{9,10},{10,1... | collective-permute-start | bytes 98312 | tf_op jit(solution)/shard_map/ppermute | solution.py:31
  53.0 3.9 %collective-permute-start.6 = (f32[2,32,1,128]{3,2,1,0:T(1,128)S(1)}, f32[2,32,1,128]{3,2,1,0:T(1,128)S(1)}, u32[]{:S(2)}, u32[]{:S(2)}) collective-permute-start(f32[2,32,1,128]{3,2,1,0:T(1,128)S(1)} %get-tuple-element.15), channel_id=1, source_target_pairs={{1,0},{2,1},{3,2},{0,3},{5,4},{6,5},{7,6},{4,7},{9,8},{10,9},{11,1... | collective-permute-start | bytes 98312 | tf_op jit(solution)/shard_map/ppermute | solution.py:32
  57.3 1.3 %copy-start.5 = (f32[32,32,127]{2,1,0:T(8,128)S(1)}, f32[32,32,127]{2,1,0:T(8,128)}, u32[]{:S(2)}) copy-start(f32[32,32,127]{2,1,0:T(8,128)} %copy-done.4) | copy-start | bytes 1560580
  57.3 1.4 %copy-start.7 = (f32[32,32,127]{2,1,0:T(8,128)S(1)}, f32[32,32,127]{2,1,0:T(8,128)}, u32[]{:S(2)}) copy-start(f32[32,32,127]{2,1,0:T(8,128)} %copy-done.6) | copy-start | bytes 1560580
  57.3 1.6 %copy-start.9 = (f32[32,32,127]{2,1,0:T(8,128)S(1)}, f32[32,32,127]{2,1,0:T(8,128)}, u32[]{:S(2)}) copy-start(f32[32,32,127]{2,1,0:T(8,128)} %copy-done.8) | copy-start | bytes 1560580
  60.1 14.3 %copy-start.14 = (pred[8]{0:T(512)(128)(4,1)S(1)}, pred[8]{0:T(512)(128)(4,1)}, u32[]{:S(2)}) copy-start(pred[8]{0:T(512)(128)(4,1)} %copy-done.13) | copy-start | bytes 28
  75.3 5.2 %collective-permute-start.7 = (f32[1,2,32,128]{3,2,1,0:T(8,128)S(1)}, f32[1,2,32,128]{3,2,1,0:T(8,128)S(1)}, u32[]{:S(2)}, u32[]{:S(2)}) collective-permute-start(f32[1,2,32,128]{3,2,1,0:T(8,128)S(1)} %bitcast.101), channel_id=1, source_target_pairs={{0,4},{4,8},{8,12},{12,16},{16,20},{20,24},{24,28},{28,0},{1,5},{5... | collective-permute-start | bytes 98312 | tf_op jit(solution)/shard_map/ppermute | solution.py:13
  80.5 5.1 %collective-permute-start.8 = (f32[1,2,32,128]{3,2,1,0:T(8,128)S(1)}, f32[1,2,32,128]{3,2,1,0:T(8,128)S(1)}, u32[]{:S(2)}, u32[]{:S(2)}) collective-permute-start(f32[1,2,32,128]{3,2,1,0:T(8,128)S(1)} %collective-permute-done.7), channel_id=1, source_target_pairs={{0,4},{4,8},{8,12},{12,16},{16,20},{20,24},{24,28},{28,0},{1,5},{5... | collective-permute-start | bytes 98312 | tf_op jit(solution)/shard_map/ppermute | solution.py:13
  85.6 5.1 %collective-permute-start.9 = (f32[1,2,32,128]{3,2,1,0:T(8,128)S(1)}, f32[1,2,32,128]{3,2,1,0:T(8,128)S(1)}, u32[]{:S(2)}, u32[]{:S(2)}) collective-permute-start(f32[1,2,32,128]{3,2,1,0:T(8,128)S(1)} %collective-permute-done.8), channel_id=1, source_target_pairs={{0,4},{4,8},{8,12},{12,16},{16,20},{20,24},{24,28},{28,0},{1,5},{5... | collective-permute-start | bytes 98312 | tf_op jit(solution)/shard_map/ppermute | solution.py:13
  90.8 5.1 %collective-permute-start.10 = (f32[1,2,32,128]{3,2,1,0:T(8,128)S(1)}, f32[1,2,32,128]{3,2,1,0:T(8,128)S(1)}, u32[]{:S(2)}, u32[]{:S(2)}) collective-permute-start(f32[1,2,32,128]{3,2,1,0:T(8,128)S(1)} %collective-permute-done.9), channel_id=1, source_target_pairs={{0,4},{4,8},{8,12},{12,16},{16,20},{20,24},{24,28},{28,0},{1,5},{5... | collective-permute-start | bytes 98312 | tf_op jit(solution)/shard_map/ppermute | solution.py:13
  95.9 5.1 %collective-permute-start.11 = (f32[1,2,32,128]{3,2,1,0:T(8,128)S(1)}, f32[1,2,32,128]{3,2,1,0:T(8,128)S(1)}, u32[]{:S(2)}, u32[]{:S(2)}) collective-permute-start(f32[1,2,32,128]{3,2,1,0:T(8,128)S(1)} %collective-permute-done.10), channel_id=1, source_target_pairs={{0,4},{4,8},{8,12},{12,16},{16,20},{20,24},{24,28},{28,0},{1,5},{5... | collective-permute-start | bytes 98312 | tf_op jit(solution)/shard_map/ppermute | solution.py:13
  101.1 5.1 %collective-permute-start.12 = (f32[1,2,32,128]{3,2,1,0:T(8,128)S(1)}, f32[1,2,32,128]{3,2,1,0:T(8,128)S(1)}, u32[]{:S(2)}, u32[]{:S(2)}) collective-permute-start(f32[1,2,32,128]{3,2,1,0:T(8,128)S(1)} %collective-permute-done.11), channel_id=1, source_target_pairs={{0,4},{4,8},{8,12},{12,16},{16,20},{20,24},{24,28},{28,0},{1,5},{5... | collective-permute-start | bytes 98312 | tf_op jit(solution)/shard_map/ppermute | solution.py:13
  106.2 5.1 %collective-permute-start.13 = (f32[1,2,32,128]{3,2,1,0:T(8,128)S(1)}, f32[1,2,32,128]{3,2,1,0:T(8,128)S(1)}, u32[]{:S(2)}, u32[]{:S(2)}) collective-permute-start(f32[1,2,32,128]{3,2,1,0:T(8,128)S(1)} %collective-permute-done.12), channel_id=1, source_target_pairs={{0,4},{4,8},{8,12},{12,16},{16,20},{20,24},{24,28},{28,0},{1,5},{5... | collective-permute-start | bytes 98312 | tf_op jit(solution)/shard_map/ppermute | solution.py:13
  (5 other events, 5.0 us)
